TPU v7x, 512 devices: a whole 4x8x8 slice. The times are simulated.
512 devices in a mesh: row: 64 (over y, z_hi, core), hid: 8 (over z_lo, x).
Axes of the slice: x: 4, y: 8, z: 8 (z_hi: 4, z_lo: 2; z = z_hi * 2 + z_lo), core: 2. Of those that a mesh axis runs over, the one named last changes fastest.
Arguments:
- features: bfloat16 [256, 256, 512], P('row'), may hold values from -6 to 6
- dw_weight: float32 [2, 7, 7, 512], replicated, may hold values from -0.875 to 0.875
- dw_bias: float32 [2, 512], replicated, may hold values from -3 to 3
- ln_gain: float32 [2, 512], replicated, may hold values from 0.1 to 1.9
- ln_bias: float32 [2, 512], replicated, may hold values from -3 to 3
- w_up: bfloat16 [2, 512, 2048], P(None, None, 'hid'), may hold values from -0.25 to 0.25
- b_up: float32 [2, 2048], P(None, 'hid'), may hold values from -3 to 3
- w_down: bfloat16 [2, 2048, 512], P(None, 'hid'), may hold values from -0.125 to 0.125
- b_down: float32 [2, 512], replicated, may hold values from -3 to 3
- layer_scale: float32 [2, 512], replicated, may hold values from 0.2 to 1
Outputs:
- result_map: bfloat16 [256, 256, 512], P('row')
All inputs are finite; a program needn't handle non-finite values.
Results may differ from a plain program's by a relative error of at most 0.018.
Values may be sent and summed in bfloat16 or wider, within the bound.
A program may use at most 64 MiB of HBM per device.

v0:
```python
import jax
import jax.numpy as jnp
from jax import lax
from jax.sharding import PartitionSpec as P


def extended(block, sides, width):
    for axis, dim in sides:
        count = lax.axis_size(axis)
        forward = [(i, i + 1) for i in range(count - 1)]
        backward = [(target, source) for source, target in forward]
        low = lax.ppermute(
            lax.slice_in_dim(block, block.shape[dim] - width, None, axis=dim), axis, forward
        )
        high = lax.ppermute(lax.slice_in_dim(block, 0, width, axis=dim), axis, backward)
        block = jnp.concatenate([low, block, high], axis=dim)
    return block


def depthwise(padded, kernel, bias):
    pad = kernel.shape[0] // 2
    rows = padded.shape[0] - 2 * pad
    width = padded.shape[1]
    wide = jnp.pad(padded, ((0, 0), (pad, pad), (0, 0)))
    total = jnp.zeros((rows, width, padded.shape[2]), jnp.float32)
    for i in range(kernel.shape[0]):
        for j in range(kernel.shape[1]):
            total = total + wide[i : i + rows, j : j + width, :].astype(jnp.float32) * kernel[i, j]
    return (total + bias).astype(jnp.bfloat16)


def expand(conv, gain, shift, w_first, b_first):
    values = conv.reshape(-1, conv.shape[2]).astype(jnp.float32)
    mean = jnp.mean(values, axis=1, keepdims=True)
    var = jnp.mean((values - mean) ** 2, axis=1, keepdims=True)
    normed = ((values - mean) / jnp.sqrt(var + 1e-06) * gain + shift).astype(jnp.bfloat16)
    return jax.nn.gelu(
        jnp.dot(normed, w_first, preferred_element_type=jnp.float32) + b_first, approximate=False
    ).astype(jnp.bfloat16)


def pointwise(conv, gain, shift, w_first, b_first, w_second):
    hidden = expand(conv, gain, shift, w_first, b_first)
    partial_sum = jnp.dot(hidden, w_second, preferred_element_type=jnp.float32)
    return partial_sum.reshape(conv.shape[0], conv.shape[1], -1)


def shards(features, dw_weight, dw_bias, ln_gain, ln_bias, w_up, b_up, w_down, b_down, layer_scale):
    reach = dw_weight.shape[1] // 2
    state = features
    for b in range(dw_weight.shape[0]):
        padded = extended(state, (("row", 0),), reach)
        conv = depthwise(padded, dw_weight[b], dw_bias[b])
        partial_sum = pointwise(conv, ln_gain[b], ln_bias[b], w_up[b], b_up[b], w_down[b])
        summed = lax.psum(partial_sum.astype(jnp.bfloat16), "hid").astype(jnp.float32)
        state = (state.astype(jnp.float32) + layer_scale[b] * (summed + b_down[b])).astype(
            jnp.bfloat16
        )
    return state


def solution(mesh):
    return jax.shard_map(
        shards,
        mesh=mesh,
        in_specs=(
            P("row", None, None),
            P(),
            P(),
            P(),
            P(),
            P(None, None, "hid"),
            P(None, "hid"),
            P(None, "hid", None),
            P(),
            P(),
        ),
        out_specs=P("row", None, None),
        check_vma=False,
    )
```

profile of v0, /device:TPU:8, one launch (start us, length us, event | category | flops | bytes accessed | tf_op | source)
XLA Modules:
  0.0 297.0 jit_solution(8753654461528168947)
XLA Ops:
  6.6 1.6 fusion.99
  8.2 2.1 collective-permute-start
  10.2 10.3 %collective-permute-start.1 = (bf16[3,256,512]{2,1,0:T(8,128)(2,1)S(1)}, bf16[3,256,512]{2,1,0:T(8,128)(2,1)S(1)}, u32[]{:S(2)}, u32[]{:S(2)}) collective-permute-start(bf16[3,256,512]{2,1,0:T(8,128)(2,1)S(1)} %get-tuple-element.14), channel_id=1, source_target_pairs={{8,0},{16,8},{24,16},{32,24},{40,32},{48,40},{56,48},{64,56},{72,6... | collective-permute-start | bytes 2359304 | tf_op jit(solution)/shard_map/ppermute | solution.py:15
  20.9 14.3 %collective-permute-done = bf16[3,256,512]{2,1,0:T(8,128)(2,1)S(1)} collective-permute-done((bf16[3,256,512]{2,1,0:T(8,128)(2,1)S(1)}, bf16[3,256,512]{2,1,0:T(8,128)(2,1)S(1)}, u32[]{:S(2)}, u32[]{:S(2)}) %collective-permute-start) | collective-permute-done | bytes 786464 | tf_op jit(solution)/shard_map/ppermute | solution.py:12
  35.4 1.9 collective-permute-done.1
  37.3 0.8 select_maximum_fusion.2
  38.2 16.1 %convert_reduce_fusion.1 = (f32[4,256]{1,0:T(4,128)S(1)}, bf16[4,256,512]{2,1,0:T(8,128)(2,1)S(1)}) fusion(f32[512]{0:T(512)S(1)} %bitcast.241, f32[512]{0:T(512)S(1)} %bitcast.171, bf16[10,262,512]{2,1,0:T(8,128)(2,1)S(1)} %select_maximum_fusion.2, f32[512]{0:T(512)S(1)} %bitcast.172, f32[512]{0:T(512)S(1)} %bitcast.173, f32[512]{0:T(512)S(1)} %bitcast.174, ...), kind=kLoop, calls=%fused_computation.13 | loop fusion | flops 78642176 | bytes 52535296 | tf_op jit(solution)/shard_map/reduce_sum | solution.py:34
  54.4 0.5 fusion.10
  55.4 2.7 fusion.68
  58.1 1.4 convolution_convert_fusion.1
  59.7 90.2 %all-reduce.5.cloned.1.call-done = bf16[4,256,512]{2,1,0:T(8,128)(2,1)} async-done(((bf16[4,256,512]{2,1,0:T(8,128)(2,1)}), bf16[4,256,512]{2,1,0:T(8,128)(2,1)}) %all-reduce.5.cloned.1.call-update) | async-done | bytes 1048592 | tf_op jit(solution)/shard_map/psum | solution.py:55
  149.9 1.6 fusion.39
  151.6 1.9 collective-permute-start.2
  153.6 6.8 %collective-permute-start.3 = (bf16[3,256,512]{2,1,0:T(8,128)(2,1)S(1)}, bf16[3,256,512]{2,1,0:T(8,128)(2,1)S(1)}, u32[]{:S(2)}, u32[]{:S(2)}) collective-permute-start(bf16[3,256,512]{2,1,0:T(8,128)(2,1)S(1)} %get-tuple-element.10), channel_id=1, source_target_pairs={{8,0},{16,8},{24,16},{32,24},{40,32},{48,40},{56,48},{64,56},{72,6... | collective-permute-start | bytes 2359304 | tf_op jit(solution)/shard_map/ppermute | solution.py:15
  160.5 14.7 %collective-permute-done.2 = bf16[3,256,512]{2,1,0:T(8,128)(2,1)S(1)} collective-permute-done((bf16[3,256,512]{2,1,0:T(8,128)(2,1)S(1)}, bf16[3,256,512]{2,1,0:T(8,128)(2,1)S(1)}, u32[]{:S(2)}, u32[]{:S(2)}) %collective-permute-start.2) | collective-permute-done | bytes 786464 | tf_op jit(solution)/shard_map/ppermute | solution.py:12
  175.2 2.7 collective-permute-done.3
  177.9 0.8 select_maximum_fusion
  178.8 16.3 %convert_reduce_fusion = (f32[4,256]{1,0:T(4,128)S(1)}, bf16[4,256,512]{2,1,0:T(8,128)(2,1)S(1)}) fusion(f32[512]{0:T(512)S(1)} %bitcast.238, f32[512]{0:T(512)S(1)} %bitcast.201, bf16[10,262,512]{2,1,0:T(8,128)(2,1)S(1)} %select_maximum_fusion, f32[512]{0:T(512)S(1)} %bitcast.202, f32[512]{0:T(512)S(1)} %bitcast.203, f32[512]{0:T(512)S(1)} %bitcast.204, ...), kind=kLoop, calls=%fused_computation.9 | loop fusion | flops 81787904 | bytes 47816704 | tf_op jit(solution)/shard_map/reduce_sum | solution.py:34
  195.0 0.5 fusion.6
  195.6 0.5 fusion.9
  196.0 2.7 fusion.71
  198.8 1.4 convolution_convert_fusion
  200.2 87.4 %all-reduce.7.cloned.1.call-done = bf16[4,256,512]{2,1,0:T(8,128)(2,1)} async-done(((bf16[4,256,512]{2,1,0:T(8,128)(2,1)}), bf16[4,256,512]{2,1,0:T(8,128)(2,1)}) %all-reduce.7.cloned.1.call-update) | async-done | bytes 1048592 | tf_op jit(solution)/shard_map/psum | solution.py:55
  287.6 2.6 fusion.65
  (47 shorter events, 1.5 us)
Async XLA Ops:
  6.5 14.0 %copy-start.2 = (f32[2,7,7,512]{3,0,2,1:T(2,128)S(1)}, f32[2,7,7,512]{3,0,2,1:T(2,128)}, u32[]{:S(2)}) copy-start(f32[2,7,7,512]{3,0,2,1:T(2,128)} %param.11) | copy-start | bytes 602116
  6.5 14.2 %copy-start.3 = (f32[2,512]{1,0:T(2,128)S(1)}, f32[2,512]{1,0:T(2,128)}, u32[]{:S(2)}) copy-start(f32[2,512]{1,0:T(2,128)} %param.12) | copy-start | bytes 12292
  6.5 14.2 %copy-start.4 = (f32[2,512]{1,0:T(2,128)S(1)}, f32[2,512]{1,0:T(2,128)}, u32[]{:S(2)}) copy-start(f32[2,512]{1,0:T(2,128)} %param.13) | copy-start | bytes 12292
  6.5 14.3 %copy-start.5 = (f32[2,512]{1,0:T(2,128)S(1)}, f32[2,512]{1,0:T(2,128)}, u32[]{:S(2)}) copy-start(f32[2,512]{1,0:T(2,128)} %param.14) | copy-start | bytes 12292
  6.5 14.3 %copy-start.8 = (f32[2,256]{1,0:T(2,128)S(1)}, f32[2,256]{1,0:T(2,128)}, u32[]{:S(2)}) copy-start(f32[2,256]{1,0:T(2,128)} %param.16) | copy-start | bytes 6148
  6.5 143.3 %all-reduce.5.cloned.1.call-start = ((), (), s32[]{:S(2)}) async-start(), calls=%async_computation | async-start | bytes 2097152 | tf_op jit(solution)/shard_map/psum | solution.py:55
  8.2 27.1 %copy-start = (bf16[4,256,512]{2,1,0:T(8,128)(2,1)S(1)}, bf16[4,256,512]{2,1,0:T(8,128)(2,1)}, u32[]{:S(2)}) copy-start(bf16[4,256,512]{2,1,0:T(8,128)(2,1)} %param.10) | copy-start | bytes 3145732
  8.2 27.0 %collective-permute-start = (bf16[3,256,512]{2,1,0:T(8,128)(2,1)S(1)}, bf16[3,256,512]{2,1,0:T(8,128)(2,1)S(1)}, u32[]{:S(2)}, u32[]{:S(2)}) collective-permute-start(bf16[3,256,512]{2,1,0:T(8,128)(2,1)S(1)} %get-tuple-element.13), channel_id=1, source_target_pairs={{0,8},{8,16},{16,24},{24,32},{32,40},{40,48},{48,56},{56,64},{64,7... | collective-permute-start | bytes 2359304 | tf_op jit(solution)/shard_map/ppermute | solution.py:12
  10.2 27.1 %collective-permute-start.1 = (bf16[3,256,512]{2,1,0:T(8,128)(2,1)S(1)}, bf16[3,256,512]{2,1,0:T(8,128)(2,1)S(1)}, u32[]{:S(2)}, u32[]{:S(2)}) collective-permute-start(bf16[3,256,512]{2,1,0:T(8,128)(2,1)S(1)} %get-tuple-element.14), channel_id=1, source_target_pairs={{8,0},{16,8},{24,16},{32,24},{40,32},{48,40},{56,48},{64,56},{72,6... | collective-permute-start | bytes 2359304 | tf_op jit(solution)/shard_map/ppermute | solution.py:15
  54.3 1.0 copy-start.9
  55.4 2.8 copy-start.1
  58.1 1.5 copy-start.6
  58.1 1.5 copy-start.7
  59.6 228.0 %all-reduce.7.cloned.1.call-start = ((), (), s32[]{:S(2)}) async-start(), calls=%async_computation.1 | async-start | bytes 2097152 | tf_op jit(solution)/shard_map/psum | solution.py:55
  151.6 23.6 %collective-permute-start.2 = (bf16[3,256,512]{2,1,0:T(8,128)(2,1)S(1)}, bf16[3,256,512]{2,1,0:T(8,128)(2,1)S(1)}, u32[]{:S(2)}, u32[]{:S(2)}) collective-permute-start(bf16[3,256,512]{2,1,0:T(8,128)(2,1)S(1)} %get-tuple-element.9), channel_id=1, source_target_pairs={{0,8},{8,16},{16,24},{24,32},{32,40},{40,48},{48,56},{56,64},{64,7... | collective-permute-start | bytes 2359304 | tf_op jit(solution)/shard_map/ppermute | solution.py:12
  153.6 24.3 %collective-permute-start.3 = (bf16[3,256,512]{2,1,0:T(8,128)(2,1)S(1)}, bf16[3,256,512]{2,1,0:T(8,128)(2,1)S(1)}, u32[]{:S(2)}, u32[]{:S(2)}) collective-permute-start(bf16[3,256,512]{2,1,0:T(8,128)(2,1)S(1)} %get-tuple-element.10), channel_id=1, source_target_pairs={{8,0},{16,8},{24,16},{32,24},{40,32},{48,40},{56,48},{64,56},{72,6... | collective-permute-start | bytes 2359304 | tf_op jit(solution)/shard_map/ppermute | solution.py:15
Sparse Core Ops, SparseCore 0:
  59.7 90.1 all-reduce.4
  200.3 87.2 all-reduce.6
where the time goes:
time: 297 us
  waiting for transfers between devices  211 us (71%)
  other arithmetic  40.2 us (14%)
  starting transfers between devices  21.1 us (7%)
  between operations  13.8 us (5%)
  matrix products  8.25 us (3%)
    psum x2, waiting for transfers between devices, shards(): lax.psum(partial_sum.astype(jnp.bfloat16), 'hid').astype(jnp.float32)  178 us
    reduce_sum x2, other arithmetic, expand(): mean = jnp.mean(values, axis=1, keepdims=True)  32.3 us
    ppermute x2, waiting for transfers between devices, extended(): lax.ppermute(lax.slice_in_dim(block, block.shape[dim] - width, None, axis...  29 us
    ppermute x2, starting transfers between devices, extended(): lax.ppermute(lax.slice_in_dim(block, 0, width, axis=dim), axis, backward)  17.1 us
  transfers between devices with their start and end apart: 6, of which 6 were waited for; matrix products, arithmetic and copies ran while one was open for 0% of the time, Pallas kernels for 0%

commit v1 on v0

--- a/solution.py
+++ b/solution.py
@@ -52,7 +52,11 @@
         padded = extended(state, (("row", 0),), reach)
         conv = depthwise(padded, dw_weight[b], dw_bias[b])
         partial_sum = pointwise(conv, ln_gain[b], ln_bias[b], w_up[b], b_up[b], w_down[b])
-        summed = lax.psum(partial_sum.astype(jnp.bfloat16), "hid").astype(jnp.float32)
+        summed = (
+            jax.lax.all_gather(partial_sum.astype(jnp.bfloat16), axis_name="hid")
+            .sum(axis=0)
+            .astype(jnp.float32)
+        )
         state = (state.astype(jnp.float32) + layer_scale[b] * (summed + b_down[b])).astype(
             jnp.bfloat16
         )

time: 297 us -> 324 us (1.091)
  the two profiles are of different devices: /device:TPU:8 before, /device:TPU:1 now
where the time goes in v1:
time: 324 us; the launch traced here: 323 us
  waiting for transfers between devices  234 us (72%)
  other arithmetic  47.3 us (15%)
  starting transfers between devices  17.4 us (5%)
  between operations  13.8 us (4%)
  matrix products  8.25 us (3%)
    all_gather x2, waiting for transfers between devices, shards(): jax.lax.all_gather(partial_sum.astype(jnp.bfloat16), axis_name='hid')  190 us
    reduce_sum x2, other arithmetic, expand(): mean = jnp.mean(values, axis=1, keepdims=True)  32.3 us
    ppermute x2, waiting for transfers between devices, extended(): lax.ppermute(lax.slice_in_dim(block, 0, width, axis=dim), axis, backward)  31.5 us
    ppermute x2, waiting for transfers between devices, extended(): lax.ppermute(lax.slice_in_dim(block, block.shape[dim] - width, None, axis...  12.3 us
    ppermute x2, starting transfers between devices, extended(): lax.ppermute(lax.slice_in_dim(block, block.shape[dim] - width, None, axis...  12.2 us
    reduce_sum x2, other arithmetic, shards(): summed = jax.lax.all_gather(partial_sum.astype(jnp.bfloat16), axis_name='...  9.51 us
  transfers between devices with their start and end apart: 6, of which 6 were waited for; matrix products, arithmetic and copies ran while one was open for 0% of the time, Pallas kernels for 0%

profile of v1, /device:TPU:1, one launch (start us, length us, event | category | flops | bytes accessed | tf_op | source)
XLA Modules:
  0.0 323.2 jit_solution(16281486637602460793)
XLA Ops:
  6.6 1.6 fusion.99
  8.2 7.3 %collective-permute-start = (bf16[3,256,512]{2,1,0:T(8,128)(2,1)S(1)}, bf16[3,256,512]{2,1,0:T(8,128)(2,1)S(1)}, u32[]{:S(2)}, u32[]{:S(2)}) collective-permute-start(bf16[3,256,512]{2,1,0:T(8,128)(2,1)S(1)} %get-tuple-element.13), channel_id=1, source_target_pairs={{0,8},{8,16},{16,24},{24,32},{32,40},{40,48},{48,56},{56,64},{64,7... | collective-permute-start | bytes 2359304 | tf_op jit(solution)/shard_map/ppermute | solution.py:12
  15.5 2.9 collective-permute-start.1
  18.9 5.6 %collective-permute-done = bf16[3,256,512]{2,1,0:T(8,128)(2,1)S(1)} collective-permute-done((bf16[3,256,512]{2,1,0:T(8,128)(2,1)S(1)}, bf16[3,256,512]{2,1,0:T(8,128)(2,1)S(1)}, u32[]{:S(2)}, u32[]{:S(2)}) %collective-permute-start) | collective-permute-done | bytes 786464 | tf_op jit(solution)/shard_map/ppermute | solution.py:12
  24.7 16.1 %collective-permute-done.1 = bf16[3,256,512]{2,1,0:T(8,128)(2,1)S(1)} collective-permute-done((bf16[3,256,512]{2,1,0:T(8,128)(2,1)S(1)}, bf16[3,256,512]{2,1,0:T(8,128)(2,1)S(1)}, u32[]{:S(2)}, u32[]{:S(2)}) %collective-permute-start.1) | collective-permute-done | bytes 786464 | tf_op jit(solution)/shard_map/ppermute | solution.py:15
  40.8 0.8 select_maximum_fusion.2
  41.8 16.1 %convert_reduce_fusion.1 = (f32[4,256]{1,0:T(4,128)S(1)}, bf16[4,256,512]{2,1,0:T(8,128)(2,1)S(1)}) fusion(f32[512]{0:T(512)S(1)} %bitcast.245, f32[512]{0:T(512)S(1)} %bitcast.175, bf16[10,262,512]{2,1,0:T(8,128)(2,1)S(1)} %select_maximum_fusion.2, f32[512]{0:T(512)S(1)} %bitcast.176, f32[512]{0:T(512)S(1)} %bitcast.177, f32[512]{0:T(512)S(1)} %bitcast.178, ...), kind=kLoop, calls=%fused_computation.13 | loop fusion | flops 78642176 | bytes 52535296 | tf_op jit(solution)/shard_map/reduce_sum | solution.py:34
  57.9 0.5 fusion.10
  58.9 2.7 fusion.68
  61.7 1.4 convolution_convert_fusion.1
  63.2 97.1 %all-gather.5.cloned.1.call-done = bf16[32,256,512]{2,1,0:T(8,128)(2,1)} async-done(((bf16[4,256,512]{2,1,0:T(8,128)(2,1)}), bf16[32,256,512]{2,1,0:T(8,128)(2,1)}) %all-gather.5.cloned.1.call-update) | async-done | bytes 8388624 | tf_op jit(solution)/shard_map/all_gather | solution.py:56
  160.3 4.8 %reduce_sum.62 = bf16[4,256,512]{2,1,0:T(8,128)(2,1)S(1)} reduce(bf16[8,4,256,512]{3,2,1,0:T(8,128)(2,1)} %bitcast.138, bf16[]{:T(256)} %constant.33.clone.1), dimensions={0}, to_apply=%region_2.3 | reduce | flops 3670016 | bytes 9437186 | tf_op jit(solution)/shard_map/reduce_sum | solution.py:57
  165.6 4.9 %collective-permute-start.2 = (bf16[3,256,512]{2,1,0:T(8,128)(2,1)S(1)}, bf16[3,256,512]{2,1,0:T(8,128)(2,1)S(1)}, u32[]{:S(2)}, u32[]{:S(2)}) collective-permute-start(bf16[3,256,512]{2,1,0:T(8,128)(2,1)S(1)} %get-tuple-element.9), channel_id=1, source_target_pairs={{0,8},{8,16},{16,24},{24,32},{32,40},{40,48},{48,56},{56,64},{64,7... | collective-permute-start | bytes 2359304 | tf_op jit(solution)/shard_map/ppermute | solution.py:12
  170.5 2.1 collective-permute-start.3
  172.7 6.7 %collective-permute-done.2 = bf16[3,256,512]{2,1,0:T(8,128)(2,1)S(1)} collective-permute-done((bf16[3,256,512]{2,1,0:T(8,128)(2,1)S(1)}, bf16[3,256,512]{2,1,0:T(8,128)(2,1)S(1)}, u32[]{:S(2)}, u32[]{:S(2)}) %collective-permute-start.2) | collective-permute-done | bytes 786464 | tf_op jit(solution)/shard_map/ppermute | solution.py:12
  179.4 15.4 %collective-permute-done.3 = bf16[3,256,512]{2,1,0:T(8,128)(2,1)S(1)} collective-permute-done((bf16[3,256,512]{2,1,0:T(8,128)(2,1)S(1)}, bf16[3,256,512]{2,1,0:T(8,128)(2,1)S(1)}, u32[]{:S(2)}, u32[]{:S(2)}) %collective-permute-start.3) | collective-permute-done | bytes 786464 | tf_op jit(solution)/shard_map/ppermute | solution.py:15
  194.8 0.8 select_maximum_fusion
  195.7 16.3 %convert_reduce_fusion = (f32[4,256]{1,0:T(4,128)S(1)}, bf16[4,256,512]{2,1,0:T(8,128)(2,1)S(1)}) fusion(f32[512]{0:T(512)S(1)} %bitcast.242, f32[512]{0:T(512)S(1)} %bitcast.224, bf16[10,262,512]{2,1,0:T(8,128)(2,1)S(1)} %select_maximum_fusion, f32[512]{0:T(512)S(1)} %bitcast.225, f32[512]{0:T(512)S(1)} %bitcast.226, f32[512]{0:T(512)S(1)} %bitcast.227, ...), kind=kLoop, calls=%fused_computation.9 | loop fusion | flops 81787904 | bytes 47816704 | tf_op jit(solution)/shard_map/reduce_sum | solution.py:34
  212.0 0.5 fusion.6
  213.0 2.7 fusion.71
  215.8 1.4 convolution_convert_fusion
  217.2 93.0 %all-gather.7.cloned.1.call-done = bf16[32,256,512]{2,1,0:T(8,128)(2,1)} async-done(((bf16[4,256,512]{2,1,0:T(8,128)(2,1)}), bf16[32,256,512]{2,1,0:T(8,128)(2,1)}) %all-gather.7.cloned.1.call-update) | async-done | bytes 8388624 | tf_op jit(solution)/shard_map/all_gather | solution.py:56
  310.2 4.8 %reduce_sum.65 = bf16[4,256,512]{2,1,0:T(8,128)(2,1)S(1)} reduce(bf16[8,4,256,512]{3,2,1,0:T(8,128)(2,1)} %bitcast.139, bf16[]{:T(256)} %constant.33.clone.1), dimensions={0}, to_apply=%region_5.6 | reduce | flops 3670016 | bytes 9437186 | tf_op jit(solution)/shard_map/reduce_sum | solution.py:57
  315.0 1.4 fusion.65
  (53 shorter events, 2.4 us)
Async XLA Ops:
  6.5 11.9 %copy-start.4 = (f32[2,512]{1,0:T(2,128)S(1)}, f32[2,512]{1,0:T(2,128)}, u32[]{:S(2)}) copy-start(f32[2,512]{1,0:T(2,128)} %param.12) | copy-start | bytes 12292
  6.5 11.9 %copy-start.5 = (f32[2,512]{1,0:T(2,128)S(1)}, f32[2,512]{1,0:T(2,128)}, u32[]{:S(2)}) copy-start(f32[2,512]{1,0:T(2,128)} %param.13) | copy-start | bytes 12292
  6.5 12.0 %copy-start.3 = (f32[2,7,7,512]{3,0,2,1:T(2,128)S(1)}, f32[2,7,7,512]{3,0,2,1:T(2,128)}, u32[]{:S(2)}) copy-start(f32[2,7,7,512]{3,0,2,1:T(2,128)} %param.11) | copy-start | bytes 602116
  6.5 12.2 %copy-start.6 = (f32[2,512]{1,0:T(2,128)S(1)}, f32[2,512]{1,0:T(2,128)}, u32[]{:S(2)}) copy-start(f32[2,512]{1,0:T(2,128)} %param.14) | copy-start | bytes 12292
  6.5 12.2 %copy-start.9 = (f32[2,256]{1,0:T(2,128)S(1)}, f32[2,256]{1,0:T(2,128)}, u32[]{:S(2)}) copy-start(f32[2,256]{1,0:T(2,128)} %param.16) | copy-start | bytes 6148
  6.5 153.7 %all-gather.5.cloned.1.call-start = ((), (), s32[]{:S(2)}) async-start(), calls=%async_computation | async-start | bytes 9437184 | tf_op jit(solution)/shard_map/all_gather | solution.py:56
  8.2 16.4 %copy-start = (bf16[4,256,512]{2,1,0:T(8,128)(2,1)S(1)}, bf16[4,256,512]{2,1,0:T(8,128)(2,1)}, u32[]{:S(2)}) copy-start(bf16[4,256,512]{2,1,0:T(8,128)(2,1)} %param.10) | copy-start | bytes 3145732
  8.2 16.3 %collective-permute-start = (bf16[3,256,512]{2,1,0:T(8,128)(2,1)S(1)}, bf16[3,256,512]{2,1,0:T(8,128)(2,1)S(1)}, u32[]{:S(2)}, u32[]{:S(2)}) collective-permute-start(bf16[3,256,512]{2,1,0:T(8,128)(2,1)S(1)} %get-tuple-element.13), channel_id=1, source_target_pairs={{0,8},{8,16},{16,24},{24,32},{32,40},{40,48},{48,56},{56,64},{64,7... | collective-permute-start | bytes 2359304 | tf_op jit(solution)/shard_map/ppermute | solution.py:12
  15.5 25.3 %collective-permute-start.1 = (bf16[3,256,512]{2,1,0:T(8,128)(2,1)S(1)}, bf16[3,256,512]{2,1,0:T(8,128)(2,1)S(1)}, u32[]{:S(2)}, u32[]{:S(2)}) collective-permute-start(bf16[3,256,512]{2,1,0:T(8,128)(2,1)S(1)} %get-tuple-element.14), channel_id=1, source_target_pairs={{8,0},{16,8},{24,16},{32,24},{40,32},{48,40},{56,48},{64,56},{72,6... | collective-permute-start | bytes 2359304 | tf_op jit(solution)/shard_map/ppermute | solution.py:15
  57.8 1.0 copy-start.10
  58.9 2.8 copy-start.1
  61.6 1.5 copy-start.7
  61.6 1.5 copy-start.8
  63.1 247.1 %all-gather.7.cloned.1.call-start = ((), (), s32[]{:S(2)}) async-start(), calls=%async_computation.1 | async-start | bytes 9437184 | tf_op jit(solution)/shard_map/all_gather | solution.py:56
  165.6 13.9 %collective-permute-start.2 = (bf16[3,256,512]{2,1,0:T(8,128)(2,1)S(1)}, bf16[3,256,512]{2,1,0:T(8,128)(2,1)S(1)}, u32[]{:S(2)}, u32[]{:S(2)}) collective-permute-start(bf16[3,256,512]{2,1,0:T(8,128)(2,1)S(1)} %get-tuple-element.9), channel_id=1, source_target_pairs={{0,8},{8,16},{16,24},{24,32},{32,40},{40,48},{48,56},{56,64},{64,7... | collective-permute-start | bytes 2359304 | tf_op jit(solution)/shard_map/ppermute | solution.py:12
  170.5 24.4 %collective-permute-start.3 = (bf16[3,256,512]{2,1,0:T(8,128)(2,1)S(1)}, bf16[3,256,512]{2,1,0:T(8,128)(2,1)S(1)}, u32[]{:S(2)}, u32[]{:S(2)}) collective-permute-start(bf16[3,256,512]{2,1,0:T(8,128)(2,1)S(1)} %get-tuple-element.10), channel_id=1, source_target_pairs={{8,0},{16,8},{24,16},{32,24},{40,32},{48,40},{56,48},{64,56},{72,6... | collective-permute-start | bytes 2359304 | tf_op jit(solution)/shard_map/ppermute | solution.py:15
  212.0 1.0 copy-start.11
  213.0 2.7 copy-start.2
Sparse Core Ops, SparseCore 0:
  63.2 96.9 all-gather.4
  217.3 92.8 all-gather.6
